TPU v7x, 32 devices: a whole 2x2x4 slice. The times are simulated.
32 devices in a mesh: survey: 2 (over x), chan: 16 (over z, y, core).
Axes of the slice: x: 2, y: 2, z: 4, core: 2. Of those that a mesh axis runs over, the one named last changes fastest.
Arguments:
- das_window: float32 [8192, 8192], P(('survey', 'chan')), parts along dimension 0, may hold values from -6 to 6
- fan_bound: int32 [4096], replicated, may hold values from -1 to 2048, as said below
- tap_offset: int32 [8, 32], replicated, may hold values from -31 to 31, as said below
- tap_weight: float32 [8, 32], replicated, may hold values from -1 to 1
Outputs:
- filtered: float32 [8192, 8192], P(('survey', 'chan')), parts along dimension 0
- energy: float32 [8192, 8, 128], P(('survey', 'chan')), parts along dimension 0
There are 2 independent parts, one for each index of `survey`. A program takes and returns all parts, laid end to end along the dimension named above; an argument that names none is the same for every part. Nothing has to cross between parts.
Inputs may be any that keep to these rules, and one draw needn't show every extreme that they name: `fan_bound`: entry f bounds the magnitude of the signed channel wavenumber bin passed at the time frequency bins +f and -f; -1 passes none. `tap_offset`: the channel offset of a tap relative to the output channel.
All inputs are finite; a program needn't handle non-finite values.
Results may differ from a plain program's by a relative error of at most 0.0027.
Values may be sent and summed in bfloat16 or wider, within the bound.
No kernel may reach another device: no remote copies, remote signals or barrier semaphores. Data moves between devices by JAX's collectives and lax.ppermute only.
A program may use at most 256 MiB of HBM per device.

v0:
```python
import math
import jax
import jax.numpy as jnp
from jax import lax
from jax.sharding import PartitionSpec as P

HALO = 31
WIN = 64
PRECISE = lax.Precision.HIGHEST


def padded_2(value, sides, width):
    for axis, dim in sides:
        peers, length = (lax.axis_size(axis), value.shape[dim])
        up = [(i, (i + 1) % peers) for i in range(peers - 1)]
        down = [(j, i) for i, j in up]
        last = lax.slice_in_dim(value, length - width, length, axis=dim)
        leading = lax.slice_in_dim(value, 0, width, axis=dim)
        before = lax.ppermute(last, axis, up)
        after = lax.ppermute(leading, axis, down)
        value = jnp.concatenate([before, value, after], axis=dim)
    return value


def split_length(length_all):
    leading = 1
    while length_all % (4 * leading) == 0 and 4 * leading * leading <= length_all:
        leading = leading * 2
    return (leading, length_all // leading)


def phases(index_product, modulus, direction):
    angle = (index_product % modulus).astype(jnp.float32) * (2.0 * math.pi / modulus)
    return (jnp.cos(angle), direction * jnp.sin(angle))


def complex_table(real_part, imag_part, q_axis):
    first_row = jnp.stack([real_part, imag_part], axis=q_axis)
    second_row = jnp.stack([-imag_part, real_part], axis=q_axis)
    return jnp.stack([first_row, second_row], axis=0)


def square_phases(leading, direction):
    left_index = lax.broadcasted_iota(jnp.int32, (leading, leading), 0)
    right_index = lax.broadcasted_iota(jnp.int32, (leading, leading), 1)
    return phases(left_index * right_index, leading, direction)


def folded_table(shape_three, bin_axis, inner_axis, leading, modulus, direction):
    bin_index = lax.broadcasted_iota(jnp.int32, shape_three, bin_axis)
    outer_index = lax.broadcasted_iota(jnp.int32, shape_three, 3 - bin_axis - inner_axis)
    inner_index = lax.broadcasted_iota(jnp.int32, shape_three, inner_axis)
    return phases(inner_index * (bin_index + leading * outer_index), modulus, direction)


def time_forward(signal, kept_bins):
    row_count, sample_count = signal.shape
    leading, trailing = split_length(sample_count)
    used_bins = kept_bins // leading
    shaped = signal.reshape(row_count, leading, trailing)
    cos_first, sin_first = square_phases(leading, -1.0)
    first_table = jnp.stack([cos_first, sin_first], axis=1)
    first = jnp.einsum("rab,apk->rpkb", shaped, first_table, precision=PRECISE)
    cos_second, sin_second = folded_table(
        (leading, trailing, used_bins), 0, 1, leading, sample_count, -1.0
    )
    second_table = complex_table(cos_second, sin_second, 2)
    out = jnp.einsum("rpkb,pkbqm->rqmk", first, second_table, precision=PRECISE)
    return out.reshape(row_count, 2, kept_bins)


def channel_transform(field, direction):
    length_all, parts_count, column_count = field.shape
    leading, trailing = split_length(length_all)
    shaped = field.reshape(leading, trailing, parts_count, column_count)
    cos_first, sin_first = square_phases(leading, direction)
    first_table = complex_table(cos_first, sin_first, 1)
    first = jnp.einsum("abpn,paqk->kbqn", shaped, first_table, precision=PRECISE)
    cos_second, sin_second = folded_table(
        (leading, trailing, trailing), 0, 1, leading, length_all, direction
    )
    second_table = complex_table(cos_second, sin_second, 2)
    out = jnp.einsum("kbpn,pkbqm->mkqn", first, second_table, precision=PRECISE)
    return out.reshape(length_all, parts_count, column_count)


def time_inverse(spectrum, sample_count):
    row_count, parts_count, bin_count = spectrum.shape
    leading, trailing = split_length(sample_count)
    used_bins = bin_count // leading
    shaped = spectrum.reshape(row_count, parts_count, used_bins, leading)
    cos_first, sin_first = folded_table(
        (leading, used_bins, trailing), 0, 2, leading, sample_count, 1.0
    )
    first_table = complex_table(cos_first, sin_first, 2)
    first = jnp.einsum("rpmk,pkmqb->rqkb", shaped, first_table, precision=PRECISE)
    cos_last, sin_last = square_phases(leading, 1.0)
    last_table = jnp.stack([cos_last, -sin_last], axis=0)
    signal = jnp.einsum("rqkb,qka->rab", first, last_table, precision=PRECISE)
    signal = signal.reshape(row_count, sample_count)
    signal = 2.0 * signal - spectrum[:, 0, 0:1]
    return signal / sample_count


def per_device(das_window, fan_bound, tap_offset, tap_weight):
    row_count, sample_count = das_window.shape
    devices = lax.axis_size("chan")
    channel_count = row_count * devices
    kept_bins = sample_count // 2
    block_bins = kept_bins // devices
    spectrum = time_forward(das_window, kept_bins)
    by_freq = lax.all_to_all(spectrum, "chan", split_axis=2, concat_axis=0, tiled=True)
    wave = channel_transform(by_freq, -1.0)
    wave_index = lax.broadcasted_iota(jnp.int32, (channel_count, 1), 0)
    wave_signed = jnp.where(wave_index < channel_count // 2, wave_index, wave_index - channel_count)
    position = lax.axis_index("chan")
    extended = jnp.concatenate([fan_bound, jnp.full((1,), -1, jnp.int32)])
    limits = lax.dynamic_slice_in_dim(extended, position * block_bins, block_bins)
    passing = (jnp.abs(wave_signed) <= limits[None, :]).astype(jnp.float32)
    back = channel_transform(wave * passing[:, None, :], 1.0) / channel_count
    by_channel = lax.all_to_all(back, "chan", split_axis=0, concat_axis=2, tiled=True)
    filtered = time_inverse(by_channel, sample_count)
    low_field = filtered.astype(jnp.bfloat16)
    padded = padded_2(low_field, (("chan", 0),), HALO)
    span_count = 2 * HALO + 1
    offsets_grid = jnp.arange(span_count, dtype=jnp.int32) - HALO
    matches = (tap_offset[:, :, None] == offsets_grid[None, None, :]).astype(jnp.float32)
    kernel_low = jnp.sum(tap_weight[:, :, None] * matches, axis=1).astype(jnp.bfloat16)
    template_count = kernel_low.shape[0]
    piece_rows = 64
    offset_index = lax.broadcasted_iota(
        jnp.int32, (span_count, piece_rows, piece_rows + 2 * HALO), 0
    )
    output_index = lax.broadcasted_iota(
        jnp.int32, (span_count, piece_rows, piece_rows + 2 * HALO), 1
    )
    input_index = lax.broadcasted_iota(
        jnp.int32, (span_count, piece_rows, piece_rows + 2 * HALO), 2
    )
    selector = (input_index - output_index == offset_index).astype(jnp.bfloat16)
    stacking = jnp.einsum("ko,ori->rki", kernel_low, selector, preferred_element_type=jnp.float32)
    stacking = stacking.astype(jnp.bfloat16).reshape(
        piece_rows * template_count, piece_rows + 2 * HALO
    )

    def one_piece(first_row):
        window_rows = lax.dynamic_slice_in_dim(padded, first_row, piece_rows + 2 * HALO, 0)
        detection = jnp.dot(stacking, window_rows, preferred_element_type=jnp.float32)
        squared = (detection * detection).reshape(
            piece_rows * template_count, sample_count // WIN, WIN
        )
        return jnp.mean(squared, axis=2).reshape(piece_rows, template_count, sample_count // WIN)

    starts = jnp.arange(0, row_count, piece_rows, dtype=jnp.int32)
    energy = lax.map(one_piece, starts).reshape(row_count, template_count, sample_count // WIN)
    return (filtered, energy)


def solution(mesh):
    return jax.shard_map(
        per_device,
        mesh=mesh,
        in_specs=(P(("survey", "chan"), None), P(), P(), P()),
        out_specs=(P(("survey", "chan"), None), P(("survey", "chan"), None, None)),
        check_vma=False,
    )
```

profile of v0, /device:TPU:17, one launch (start us, length us, event | category | flops | bytes accessed | tf_op | source)
XLA Modules:
  0.0 740.6 jit_solution(12700331765586824724)
XLA Ops:
  0.8 8.4 %sine_multiply_fusion = (f32[64,128,1,64]{1,3,2,0:T(8,128)S(1)}, f32[64,128,1,64]{1,3,2,0:T(8,128)S(1)}, f32[64,128,1,64]{1,3,2,0:T(8,128)S(1)}) fusion(s32[64]{0:T(128)S(1)} %iota_multiply_fusion.1), kind=kLoop, calls=%fused_computation.74 | loop fusion | flops 8912896 | bytes 6291712 | tf_op jit(solution)/shard_map/mul | solution.py:34
  9.2 5.0 copy.102
  14.3 4.3 maximum_bitcast_fusion.2
  18.6 16.0 %convolution_bitcast_fusion.1 = f32[256,2,64,128,1]{3,2,0,1,4:T(8,128)} fusion(f32[256,64,128,1]{2,1,0,3:T(8,128)S(1)} %bitcast.148, f32[64,1,64]{0,2,1:T(8,128)S(1)} %get-tuple-element.68, f32[64,1,64]{0,2,1:T(8,128)S(1)} %get-tuple-element.67), kind=kOutput, calls=%fused_computation.37 | convolution fusion | flops 3221233664 | bytes 25198592 | tf_op jit(solution)/shard_map/rab,apk->rpkb/dot_general | solution.py:63
  34.6 33.7 %fusion.37 = f32[256,2,64,64]{0,2,1,3:T(8,128)S(1)} fusion(f32[256,2,64,128,1]{3,2,0,1,4:T(8,128)} %convolution_bitcast_fusion.1, f32[1,64,128,2,64]{2,4,0,3,1:T(8,128)} %get-tuple-element.51, f32[1,64,128,2,64]{2,4,0,3,1:T(8,128)} %get-tuple-element.50), kind=kOutput, calls=%fused_computation.54 | convolution fusion | flops 6444548096 | bytes 33554432 | tf_op jit(solution)/shard_map/rpkb,pkbqm->rqmk/dot_general | solution.py:68
  68.3 4.9 copy.56
  73.1 23.4 %copy.57 = f32[256,2,4096]{0,1,2:T(2,128)} copy(f32[256,2,4096]{0,2,1:T(8,128)S(1)} %bitcast.153) | data formatting | bytes 16777216 | tf_op jit(solution)/shard_map/reshape | solution.py:69
  96.6 6.9 all-to-all-start
  104.0 2.3 compare_convert_fusion
  106.3 8.5 %broadcast_multiply_fusion.1 = (f32[64,64,1,64]{1,3,0,2:T(8,128)S(1)}, f32[64,64,1,64]{1,3,0,2:T(8,128)S(1)}, f32[64,64,1,64]{1,3,0,2:T(8,128)S(1)}, f32[64,64,1,64]{1,3,0,2:T(8,128)S(1)}, f32[64,64,1,64]{1,3,0,2:T(8,128)S(1)}) fusion(s32[64]{0:T(128)S(1)} %iota_multiply_fusion.1), kind=kLoop, calls=%fused_computation.83 | loop fusion | flops 4718592 | bytes 5243136 | tf_op jit(solution)/shard_map/mul | solution.py:34
  114.8 7.4 fusion.30
  122.1 163.3 %all-to-all-done = f32[256,2,4096]{0,1,2:T(2,128)} async-done(((f32[256,2,4096]{0,1,2:T(2,128)}), f32[256,2,4096]{0,1,2:T(2,128)}, u32[]{:S(2)}, u32[]{:S(2)}) %all-to-all-start) | async-done | bytes 8388640 | tf_op jit(solution)/shard_map/all_to_all | solution.py:112
  285.4 7.4 %copy.58 = f32[256,2,4096]{0,2,1:T(8,128)} copy(f32[256,2,4096]{0,1,2:T(2,128)} %all-to-all-done) | data formatting | bytes 16777216 | tf_op jit(solution)/shard_map/all_to_all | solution.py:112
  292.9 8.7 %copy.59 = f32[16,256,2,256]{3,1,0,2:T(8,128)} copy(f32[16,256,2,256]{1,3,0,2:T(8,128)} %bitcast.154) | data formatting | bytes 16777216 | tf_op jit(solution)/shard_map/all_to_all | solution.py:112
  301.6 17.6 %fusion.31 = f32[64,64,2,256,1]{3,0,1,2,4:T(8,128)} fusion(f32[64,64,2,256]{3,1,0,2:T(8,128)} %bitcast.152, f32[1,64,2,64]{1,3,2,0:T(8,128)S(1)} %get-tuple-element.53, f32[1,64,2,64]{1,3,2,0:T(8,128)S(1)} %get-tuple-element.54), kind=kOutput, calls=%fused_computation.52 | convolution fusion | flops 3221241856 | bytes 16842752 | tf_op jit(solution)/shard_map/abpn,paqk->kbqn/dot_general | solution.py:78
  319.2 22.0 %fusion.20 = f32[64,2,64,256,1]{3,2,1,0,4:T(8,128)} fusion(f32[64,64,2,256,1]{3,0,1,2,4:T(8,128)} %fusion.31, f32[1,64,64,2,64]{2,4,1,3,0:T(8,128)} %get-tuple-element.47, f32[1,64,64,2,64]{2,4,1,3,0:T(8,128)} %get-tuple-element.46), kind=kOutput, calls=%fused_computation.30 | convolution fusion | flops 3222274048 | bytes 20971520 | tf_op jit(solution)/shard_map/kbpn,pkbqm->mkqn/dot_general | solution.py:83
  341.3 11.9 %fusion.34 = f32[64,64,2,256,1]{3,0,1,2,4:T(8,128)} fusion(f32[64,2,64,256,1]{3,2,1,0,4:T(8,128)} %fusion.20, f32[64,64,256]{2,0,1:T(8,128)S(1)} %copy-done.1, f32[1,64,2,64]{1,3,2,0:T(8,128)S(1)} %get-tuple-element.55, f32[1,64,2,64]{1,3,2,0:T(8,128)S(1)} %get-tuple-element.52), kind=kOutput, calls=%fused_computation.53 | convolution fusion | flops 3223339008 | bytes 21037056 | tf_op jit(solution)/shard_map/abpn,paqk->kbqn/dot_general | solution.py:78
  353.2 22.1 %fusion.8 = f32[64,2,64,256,1]{3,2,0,1,4:T(8,128)} fusion(f32[1,64,64,2,64]{2,4,1,3,0:T(8,128)} %get-tuple-element.48, f32[1,64,64,2,64]{2,4,1,3,0:T(8,128)} %get-tuple-element.49, f32[64,64,2,256,1]{3,0,1,2,4:T(8,128)} %fusion.34), kind=kOutput, calls=%fused_computation.14 | convolution fusion | flops 3222274048 | bytes 20971520 | tf_op jit(solution)/shard_map/kbpn,pkbqm->mkqn/dot_general | solution.py:83
  375.3 4.3 fusion.16
  379.6 4.9 copy.67
  384.4 23.4 %copy.68 = f32[4096,2,256]{2,1,0:T(2,128)} copy(f32[4096,2,256]{2,0,1:T(8,128)S(1)} %bitcast.155) | data formatting | bytes 16777216 | tf_op jit(solution)/shard_map/div | solution.py:120
  407.9 5.2 all-to-all-start.1
  413.2 8.4 %fusion.55 = (f32[64,64,1,128]{3,1,2,0:T(8,128)S(1)}, f32[64,64,1,128]{3,1,2,0:T(8,128)S(1)}, f32[64,64,1,128]{3,1,2,0:T(8,128)S(1)}) fusion(s32[64]{0:T(128)S(1)} %iota_multiply_fusion.1), kind=kLoop, calls=%fused_computation.79 | loop fusion | flops 8388608 | bytes 6291712 | tf_op jit(solution)/shard_map/sin | solution.py:34
  421.7 4.2 maximum_bitcast_fusion
  425.9 169.3 %all-to-all-done.1 = f32[4096,2,256]{2,1,0:T(2,128)} async-done(((f32[4096,2,256]{2,1,0:T(2,128)}), f32[4096,2,256]{2,1,0:T(2,128)}, u32[]{:S(2)}, u32[]{:S(2)}) %all-to-all-start.1) | async-done | bytes 8388640 | tf_op jit(solution)/shard_map/all_to_all | solution.py:121
  595.2 7.4 %copy.69 = f32[4096,2,256]{2,0,1:T(8,128)} copy(f32[4096,2,256]{2,1,0:T(2,128)} %all-to-all-done.1) | data formatting | bytes 16777216 | tf_op jit(solution)/shard_map/all_to_all | solution.py:121
  602.6 8.7 %copy.70 = f32[256,2,16,256]{0,3,2,1:T(8,128)} copy(f32[256,2,16,256]{3,0,2,1:T(8,128)} %bitcast.156) | data formatting | bytes 16777216 | tf_op jit(solution)/shard_map/all_to_all | solution.py:121
  611.3 31.8 %convolution_bitcast_fusion = f32[256,2,64,128]{0,3,1,2:T(8,128)} fusion(f32[1,64,64,2,128]{4,2,0,3,1:T(8,128)} %get-tuple-element.45, f32[1,64,64,2,128]{4,2,0,3,1:T(8,128)} %get-tuple-element.44, f32[256,2,64,64,1]{0,3,2,1,4:T(8,128)} %bitcast.149), kind=kOutput, calls=%fused_computation.8 | convolution fusion | flops 6444548096 | bytes 33554432 | tf_op jit(solution)/shard_map/rpmk,pkmqb->rqkb/dot_general | solution.py:96
  643.1 16.8 %copy.72 = f32[256,2,64,128]{3,2,1,0:T(8,128)} copy(f32[256,2,64,128]{0,3,1,2:T(8,128)} %convolution_bitcast_fusion) | data formatting | bytes 33554432 | tf_op jit(solution)/shard_map/rpmk,pkmqb->rqkb/transpose | solution.py:96
  659.9 0.7 slice.12
  660.6 12.2 %bitcast_multiply_fusion.1 = f32[64,256,128]{2,0,1:T(8,128)S(1)} fusion(f32[256,2,64,128]{3,2,1,0:T(8,128)} %copy.72, f32[1,64,64]{1,2,0:T(8,128)S(1)} %get-tuple-element.71, f32[1,64,64]{1,2,0:T(8,128)S(1)} %get-tuple-element.72), kind=kOutput, calls=%fused_computation.23 | convolution fusion | flops 3223330816 | bytes 25198592 | tf_op jit(solution)/shard_map/rqkb,qka->rab/dot_general | solution.py:99
  672.8 11.9 %fusion.98 = (bf16[256,8192]{1,0:T(8,128)(2,1)S(1)}, f32[256,8192]{1,0:T(8,128)}) fusion(f32[256]{0:T(256)S(1)} %bitcast.158, f32[32,8,64,128]{3,2,1,0:T(8,128)S(1)} %bitcast.151), kind=kLoop, calls=%fused_computation.144 | loop fusion | flops 6291456 | bytes 20972544 | tf_op jit(solution)/shard_map/convert_element_type | solution.py:123
  684.7 2.0 copy-done
  686.8 2.0 collective-permute-start
  688.9 2.7 collective-permute-start.1
  692.2 8.4 %collective-permute-done = bf16[31,8192]{1,0:T(8,128)(2,1)S(1)} collective-permute-done((bf16[31,8192]{1,0:T(8,128)(2,1)S(1)}, bf16[31,8192]{1,0:T(8,128)(2,1)S(1)}, u32[]{:S(2)}, u32[]{:S(2)}) %collective-permute-start) | collective-permute-done | bytes 507936 | tf_op jit(solution)/shard_map/ppermute | solution.py:19
  700.6 3.4 collective-permute-done.1
  704.0 6.4 pad_maximum_fusion.1
  710.4 29.7 %while.10 = (s32[]{:T(128)}, f32[4,64,8,128]{3,2,1,0:T(8,128)}, s32[4]{0:T(128)S(1)}, bf16[318,8192]{1,0:T(8,128)(2,1)}, bf16[512,126]{1,0:T(8,128)(2,1)S(1)}, /*index=5*/s32[]{:T(128)}, s32[]{:T(128)}, s32[]{:T(128)}) while((s32[]{:T(128)}, f32[4,64,8,128]{3,2,1,0:T(8,128)}, s32[4]{0:T(128)S(1)}, bf16[318,8192]{1,0:T(8,128)(2,1)}, ...), condition=%wide.region_3.4_spmd, body=%wide.region_1.3_spmd.sunk | while | flops 1065353216 | bytes 4061831 | solution.py:155
  710.4 0.6 dynamic_slice.22
  712.9 4.0 bitcast_reduce_fusion.2
  717.1 0.7 bitcast_dynamic-update-slice_fusion.2
  720.4 4.1 bitcast_reduce_fusion.2
  724.6 0.7 bitcast_dynamic-update-slice_fusion.2
  727.8 4.0 bitcast_reduce_fusion.2
  732.0 0.7 bitcast_dynamic-update-slice_fusion.2
  735.2 4.0 bitcast_reduce_fusion.2
  739.4 0.7 bitcast_dynamic-update-slice_fusion.2
  (34 shorter events, 4.0 us)
Async XLA Ops:
  96.6 7.0 copy-start.2
  96.6 188.8 %all-to-all-start = ((f32[256,2,4096]{0,1,2:T(2,128)}), f32[256,2,4096]{0,1,2:T(2,128)}, u32[]{:S(2)}, u32[]{:S(2)}) async-start(f32[256,2,4096]{0,1,2:T(2,128)} %copy.57), calls=%async_computation | async-start | bytes 16777216 | tf_op jit(solution)/shard_map/all_to_all | solution.py:112
  319.2 22.1 %copy-start.1 = (f32[64,64,256]{2,0,1:T(8,128)S(1)}, f32[64,64,256]{2,0,1:T(8,128)}, u32[]{:S(2)}) copy-start(f32[64,64,256]{2,0,1:T(8,128)} %compare_convert_fusion) | copy-start | bytes 12582916
  407.9 187.3 %all-to-all-start.1 = ((f32[4096,2,256]{2,1,0:T(2,128)}), f32[4096,2,256]{2,1,0:T(2,128)}, u32[]{:S(2)}, u32[]{:S(2)}) async-start(f32[4096,2,256]{2,1,0:T(2,128)} %copy.68), calls=%async_computation.1 | async-start | bytes 16777216 | tf_op jit(solution)/shard_map/all_to_all | solution.py:121
  672.8 18.8 %copy-start.3 = (f32[8,32]{1,0:T(8,128)S(1)}, f32[8,32]{1,0:T(8,128)}, u32[]{:S(2)}) copy-start(f32[8,32]{1,0:T(8,128)} %param.9) | copy-start | bytes 3076
  672.8 18.8 %copy-start.4 = (s32[8,32]{1,0:T(8,128)S(1)}, s32[8,32]{1,0:T(8,128)}, u32[]{:S(2)}) copy-start(s32[8,32]{1,0:T(8,128)} %param.8) | copy-start | bytes 3076
  684.7 2.0 copy-start
  686.8 13.8 %collective-permute-start = (bf16[31,8192]{1,0:T(8,128)(2,1)S(1)}, bf16[31,8192]{1,0:T(8,128)(2,1)S(1)}, u32[]{:S(2)}, u32[]{:S(2)}) collective-permute-start(bf16[31,8192]{1,0:T(8,128)(2,1)S(1)} %get-tuple-element.42), channel_id=1, source_target_pairs={{0,1},{1,2},{2,3},{3,4},{4,5},{5,6},{6,7},{7,8},{8,9},{9,10},{10,1... | collective-permute-start | bytes 1523720 | tf_op jit(solution)/shard_map/ppermute | solution.py:19
  688.9 15.2 %collective-permute-start.1 = (bf16[31,8192]{1,0:T(8,128)(2,1)S(1)}, bf16[31,8192]{1,0:T(8,128)(2,1)S(1)}, u32[]{:S(2)}, u32[]{:S(2)}) collective-permute-start(bf16[31,8192]{1,0:T(8,128)(2,1)S(1)} %get-tuple-element.43), channel_id=1, source_target_pairs={{1,0},{2,1},{3,2},{4,3},{5,4},{6,5},{7,6},{8,7},{9,8},{10,9},{11,1... | collective-permute-start | bytes 1523720 | tf_op jit(solution)/shard_map/ppermute | solution.py:20
where the time goes:
time: 750 us; the launch traced here: 741 us
  waiting for transfers between devices  344 us (46%)
  matrix products  184 us (25%)
  local copies, waits for them, and re-layouts  120 us (16%)
  other arithmetic  67 us (9%)
  starting transfers between devices  16.9 us (2%)
  loops' own time  7.54 us (1%)
    all_to_all x1, waiting for transfers between devices, per_device(): lax.all_to_all(back, 'chan', split_axis=0, concat_axis=2, tiled=True)  169 us
    all_to_all x1, waiting for transfers between devices, per_device(): lax.all_to_all(spectrum, 'chan', split_axis=2, concat_axis=0, tiled=True)  163 us
    dot_general x2, matrix products, channel_transform(): out = jnp.einsum('kbpn,pkbqm->mkqn', first, second_table, precision=PRECISE)  44.2 us
    dot_general x1, matrix products, time_forward(): out = jnp.einsum('rpkb,pkbqm->rqmk', first, second_table, precision=PRECISE)  33.7 us
    dot_general x1, matrix products, time_inverse(): jnp.einsum('rpmk,pkmqb->rqkb', shaped, first_table, precision=PRECISE)  31.8 us
    dot_general x2, matrix products, channel_transform(): jnp.einsum('abpn,paqk->kbqn', shaped, first_table, precision=PRECISE)  29.5 us
    div x2, local copies, waits for them, and re-layouts, per_device(): back = channel_transform(wave * passing[:, None, :], 1.0) / channel_count  28.3 us
    reshape x1, local copies, waits for them, and re-layouts, time_forward(): return out.reshape(row_count, 2, kept_bins)  23.4 us
  transfers between devices with their start and end apart: 4, of which 4 were waited for; matrix products, arithmetic and copies ran while one was open for 4% of the time, Pallas kernels for 0%

commit v1 on v0

--- a/solution.py
+++ b/solution.py
@@ -3,10 +3,25 @@
 import jax.numpy as jnp
 from jax import lax
 from jax.sharding import PartitionSpec as P
+from jax.lax import axis_index, ppermute, psum
 
 HALO = 31
 WIN = 64
 PRECISE = lax.Precision.HIGHEST
+
+
+def _match_cubes(u_in, array_axis, s0):
+    step_out = u_in.shape
+    b_next = u_in.reshape(
+        *step_out[:array_axis], s0, step_out[array_axis] // s0, *step_out[array_axis + 1 :]
+    )
+    return jnp.moveaxis(b_next, array_axis, 0)
+
+
+def _meet_turns(w_in, axis_k):
+    block_next = list(w_in.shape[1:])
+    block_next[axis_k] *= w_in.shape[0]
+    return jnp.moveaxis(w_in, 0, axis_k).reshape(block_next)
 
 
 def padded_2(value, sides, width):
@@ -109,7 +124,16 @@
     kept_bins = sample_count // 2
     block_bins = kept_bins // devices
     spectrum = time_forward(das_window, kept_bins)
-    by_freq = lax.all_to_all(spectrum, "chan", split_axis=2, concat_axis=0, tiled=True)
+    res, w2 = (psum(1, axis_name="chan"), axis_index("chan"))
+    placed = _match_cubes(spectrum, 2, res)
+    buffers = [placed[w2]]
+    for rr in tuple(range(1, res)):
+        local_part = placed[w2 ^ rr]
+        buffers.append(
+            ppermute(local_part, axis_name="chan", perm=[(i0, i0 ^ rr) for i0 in range(res)])
+        )
+    placed = jnp.stack(buffers, axis=0)[w2 ^ jnp.arange(res)]
+    by_freq = _meet_turns(placed, 0)
     wave = channel_transform(by_freq, -1.0)
     wave_index = lax.broadcasted_iota(jnp.int32, (channel_count, 1), 0)
     wave_signed = jnp.where(wave_index < channel_count // 2, wave_index, wave_index - channel_count)

time: 750 us -> 776 us (1.035)
  starting transfers between devices: 16.9 us -> 35.7 us
  local copies, waits for them, and re-layouts: 120 us -> 137 us
  waiting for transfers between devices: 344 us -> 332 us
    all_to_all x1 -> x0, waiting for transfers between devices: 163 us -> none  [per_device(): lax.all_to_all(spectrum, 'chan', split_axis=2, concat_axis=0, tiled=True)]
    ppermute x0 -> x15, waiting for transfers between devices: none -> 152 us  [per_device(): ppermute(local_part, axis_name='chan', perm=[(i0, i0 ^ rr) for i0 in rang...]
    ppermute x0 -> x15, starting transfers between devices: none -> 26.3 us  [per_device(): ppermute(local_part, axis_name='chan', perm=[(i0, i0 ^ rr) for i0 in rang...]
    reshape x1 -> x0, local copies, waits for them, and re-layouts: 23.4 us -> none  [time_forward(): return out.reshape(row_count, 2, kept_bins)]
    another operation x0 -> x18, local copies, waits for them, and re-layouts: none -> 23.3 us
    unnamed x11 -> x40, local copies, waits for them, and re-layouts: 7.04 us -> 25.9 us
    all_to_all x2 -> x0, local copies, waits for them, and re-layouts: 16.2 us -> none  [per_device(): lax.all_to_all(spectrum, 'chan', split_axis=2, concat_axis=0, tiled=True)]
    gather x0 -> x2, local copies, waits for them, and re-layouts: none -> 11.7 us  [per_device(): placed = jnp.stack(buffers, axis=0)[w2 ^ jnp.arange(res)]]
  transfers between devices with their start and end apart: 4 -> 18, of which waited for: 4 -> 12; matrix products, arithmetic and copies ran while one was open for 4% -> 9% of each run, Pallas kernels for 0% -> 0%
where the time goes in v1:
time: 776 us; the launch traced here: 766 us
  waiting for transfers between devices  332 us (43%)
  matrix products  180 us (23%)
  local copies, waits for them, and re-layouts  137 us (18%)
  other arithmetic  71.3 us (9%)
  starting transfers between devices  35.7 us (5%)
  loops' own time  8.4 us (1%)
    all_to_all x1, waiting for transfers between devices, per_device(): lax.all_to_all(back, 'chan', split_axis=0, concat_axis=2, tiled=True)  169 us
    ppermute x15, waiting for transfers between devices, per_device(): ppermute(local_part, axis_name='chan', perm=[(i0, i0 ^ rr) for i0 in rang...  152 us
    dot_general x2, matrix products, channel_transform(): out = jnp.einsum('kbpn,pkbqm->mkqn', first, second_table, precision=PRECISE)  44.3 us
    dot_general x1, matrix products, time_forward(): out = jnp.einsum('rpkb,pkbqm->rqmk', first, second_table, precision=PRECISE)  33.7 us
    dot_general x1, matrix products, time_inverse(): jnp.einsum('rpmk,pkmqb->rqkb', shaped, first_table, precision=PRECISE)  31.7 us
    div x2, local copies, waits for them, and re-layouts, per_device(): back = channel_transform(wave * passing[:, None, :], 1.0) / channel_count  28.3 us
    ppermute x15, starting transfers between devices, per_device(): ppermute(local_part, axis_name='chan', perm=[(i0, i0 ^ rr) for i0 in rang...  26.3 us
    unnamed x40, local copies, waits for them, and re-layouts  25.9 us
  transfers between devices with their start and end apart: 18, of which 12 were waited for; matrix products, arithmetic and copies ran while one was open for 9% of the time, Pallas kernels for 0%

profile of v1, /device:TPU:17, one launch (start us, length us, event | category | flops | bytes accessed | tf_op | source)
XLA Modules:
  0.0 765.9 jit_solution(6404005559477305063)
XLA Ops:
  0.9 8.4 %sine_multiply_fusion = (f32[64,128,1,64]{1,3,2,0:T(8,128)S(1)}, f32[64,128,1,64]{1,3,2,0:T(8,128)S(1)}, f32[64,128,1,64]{1,3,2,0:T(8,128)S(1)}) fusion(s32[64]{0:T(128)S(1)} %iota_multiply_fusion.1), kind=kLoop, calls=%fused_computation.75 | loop fusion | flops 8912896 | bytes 6291712 | tf_op jit(solution)/shard_map/mul | solution.py:49
  9.3 5.0 copy.191
  14.3 4.3 maximum_bitcast_fusion.2
  18.7 16.0 %convolution_bitcast_fusion.1 = f32[256,2,64,128,1]{3,2,0,1,4:T(8,128)} fusion(f32[256,64,128,1]{2,1,0,3:T(8,128)S(1)} %bitcast.194, f32[64,1,64]{0,2,1:T(8,128)S(1)} %get-tuple-element.84, f32[64,1,64]{0,2,1:T(8,128)S(1)} %get-tuple-element.83), kind=kOutput, calls=%fused_computation.38 | convolution fusion | flops 3221233664 | bytes 25198592 | tf_op jit(solution)/shard_map/rab,apk->rpkb/dot_general | solution.py:78
  34.7 33.7 %fusion.37 = f32[256,2,64,64]{0,2,1,3:T(8,128)S(1)} fusion(f32[256,2,64,128,1]{3,2,0,1,4:T(8,128)} %convolution_bitcast_fusion.1, f32[1,64,128,2,64]{2,4,0,3,1:T(8,128)} %get-tuple-element.67, f32[1,64,128,2,64]{2,4,0,3,1:T(8,128)} %get-tuple-element.66), kind=kOutput, calls=%fused_computation.55 | convolution fusion | flops 6444548096 | bytes 33554432 | tf_op jit(solution)/shard_map/rpkb,pkbqm->rqmk/dot_general | solution.py:83
  68.4 8.3 %copy.131 = f32[256,2,64,64]{0,3,2,1:T(8,128)} copy(f32[256,2,64,64]{0,2,1,3:T(8,128)S(1)} %fusion.37) | data formatting | bytes 16777216 | tf_op jit(solution)/shard_map/rpkb,pkbqm->rqmk/transpose | solution.py:83
  76.6 5.9 constant_dynamic-slice_fusion
  91.7 10.2 %broadcast_multiply_fusion.1 = (f32[64,64,1,64]{1,3,0,2:T(8,128)S(1)}, f32[64,64,1,64]{1,3,0,2:T(8,128)}, f32[64,64,1,64]{1,3,0,2:T(8,128)}, f32[64,64,1,64]{1,3,0,2:T(8,128)}, f32[64,64,1,64]{1,3,0,2:T(8,128)}) fusion(s32[64]{0:T(128)S(1)} %iota_multiply_fusion.1), kind=kLoop, calls=%fused_computation.84 | loop fusion | flops 4718592 | bytes 5243136 | tf_op jit(solution)/shard_map/mul | solution.py:49
  107.8 9.6 %fusion.30 = (f32[1,64,64,2,64]{2,4,1,3,0:T(8,128)}, f32[1,64,64,2,64]{2,4,1,3,0:T(8,128)}, f32[1,64,64,2,64]{2,4,1,3,0:T(8,128)}, f32[1,64,64,2,64]{2,4,1,3,0:T(8,128)}) fusion(f32[64,64,1,64]{1,3,0,2:T(8,128)} %get-tuple-element.79, f32[64,64,1,64]{1,3,0,2:T(8,128)S(1)} %get-tuple-element.75, f32[64,64,1,64]{1,3,0,2:T(8,128)S(1)} %copy-done.2, ...), kind=kLoop, calls=%fused_computation.47 | loop fusion | flops 2097152 | bytes 13631488 | tf_op jit(solution)/shard_map/stack | solution.py:55
  143.9 14.3 %collective-permute-done.5 = f32[256,2,256]{2,0,1:T(8,128)S(1)} collective-permute-done((f32[256,2,256]{2,0,1:T(8,128)}, f32[256,2,256]{2,0,1:T(8,128)S(1)}, u32[]{:S(2)}, u32[]{:S(2)}) %collective-permute-start.5) | collective-permute-done | bytes 524320 | tf_op jit(solution)/shard_map/ppermute | solution.py:133
  158.3 5.1 collective-permute-start.10
  164.2 5.3 collective-permute-done.6
  173.6 51.2 %collective-permute-done.8 = f32[256,2,256]{2,0,1:T(8,128)S(1)} collective-permute-done((f32[256,2,256]{2,0,1:T(8,128)}, f32[256,2,256]{2,0,1:T(8,128)S(1)}, u32[]{:S(2)}, u32[]{:S(2)}) %collective-permute-start.8) | collective-permute-done | bytes 524320 | tf_op jit(solution)/shard_map/ppermute | solution.py:133
  224.7 3.3 collective-permute-start.13
  228.9 18.3 %collective-permute-done.9 = f32[256,2,256]{2,0,1:T(8,128)S(1)} collective-permute-done((f32[256,2,256]{2,0,1:T(8,128)}, f32[256,2,256]{2,0,1:T(8,128)S(1)}, u32[]{:S(2)}, u32[]{:S(2)}) %collective-permute-start.9) | collective-permute-done | bytes 524320 | tf_op jit(solution)/shard_map/ppermute | solution.py:133
  247.2 4.9 collective-permute-start.14
  253.0 16.6 %collective-permute-done.10 = f32[256,2,256]{2,0,1:T(8,128)S(1)} collective-permute-done((f32[256,2,256]{2,0,1:T(8,128)S(1)}, f32[256,2,256]{2,0,1:T(8,128)S(1)}, u32[]{:S(2)}, u32[]{:S(2)}) %collective-permute-start.10) | collective-permute-done | bytes 524320 | tf_op jit(solution)/shard_map/ppermute | solution.py:133
  270.4 13.5 %collective-permute-done.11 = f32[256,2,256]{2,0,1:T(8,128)S(1)} collective-permute-done((f32[256,2,256]{2,0,1:T(8,128)S(1)}, f32[256,2,256]{2,0,1:T(8,128)S(1)}, u32[]{:S(2)}, u32[]{:S(2)}) %collective-permute-start.11) | collective-permute-done | bytes 524320 | tf_op jit(solution)/shard_map/ppermute | solution.py:133
  284.8 11.4 %collective-permute-done.12 = f32[256,2,256]{2,0,1:T(8,128)S(1)} collective-permute-done((f32[256,2,256]{2,0,1:T(8,128)S(1)}, f32[256,2,256]{2,0,1:T(8,128)S(1)}, u32[]{:S(2)}, u32[]{:S(2)}) %collective-permute-start.12) | collective-permute-done | bytes 524320 | tf_op jit(solution)/shard_map/ppermute | solution.py:133
  297.0 10.4 %collective-permute-done.13 = f32[256,2,256]{2,0,1:T(8,128)S(1)} collective-permute-done((f32[256,2,256]{2,0,1:T(8,128)S(1)}, f32[256,2,256]{2,0,1:T(8,128)S(1)}, u32[]{:S(2)}, u32[]{:S(2)}) %collective-permute-start.13) | collective-permute-done | bytes 524320 | tf_op jit(solution)/shard_map/ppermute | solution.py:133
  308.2 10.8 %collective-permute-done.14 = f32[256,2,256]{2,0,1:T(8,128)S(1)} collective-permute-done((f32[256,2,256]{2,0,1:T(8,128)S(1)}, f32[256,2,256]{2,0,1:T(8,128)S(1)}, u32[]{:S(2)}, u32[]{:S(2)}) %collective-permute-start.14) | collective-permute-done | bytes 524320 | tf_op jit(solution)/shard_map/ppermute | solution.py:133
  319.8 7.7 %gather_fusion = f32[16,256,2,256]{3,1,2,0:T(8,128)} fusion(f32[16,256,2,256]{3,1,2,0:T(8,128)} %bitcast_dynamic-update-slice_fusion.1, s32[1024]{0:T(1024)S(1)} %pad_clamp_fusion), kind=kCustom, calls=%fused_computation | custom fusion | bytes 16777280 | tf_op jit(solution)/shard_map/gather | solution.py:135
  327.5 3.9 copy.148
  331.4 13.2 %fusion.31 = f32[64,64,2,256,1]{3,0,1,2,4:T(8,128)} fusion(f32[64,64,2,256]{3,1,0,2:T(8,128)S(1)} %bitcast.199, f32[1,64,2,64]{1,3,2,0:T(8,128)S(1)} %get-tuple-element.69, f32[1,64,2,64]{1,3,2,0:T(8,128)S(1)} %get-tuple-element.70), kind=kOutput, calls=%fused_computation.53 | convolution fusion | flops 3221241856 | bytes 16842752 | tf_op jit(solution)/shard_map/abpn,paqk->kbqn/dot_general | solution.py:93
  344.7 22.1 %fusion.20 = f32[64,2,64,256,1]{3,2,1,0,4:T(8,128)} fusion(f32[64,64,2,256,1]{3,0,1,2,4:T(8,128)} %fusion.31, f32[1,64,64,2,64]{2,4,1,3,0:T(8,128)} %get-tuple-element.63, f32[1,64,64,2,64]{2,4,1,3,0:T(8,128)} %get-tuple-element.62), kind=kOutput, calls=%fused_computation.31 | convolution fusion | flops 3222274048 | bytes 20971520 | tf_op jit(solution)/shard_map/kbpn,pkbqm->mkqn/dot_general | solution.py:98
  366.8 11.9 %fusion.34 = f32[64,64,2,256,1]{3,0,1,2,4:T(8,128)} fusion(f32[64,2,64,256,1]{3,2,1,0,4:T(8,128)} %fusion.20, f32[64,64,256]{2,0,1:T(8,128)S(1)} %copy-done.1, f32[1,64,2,64]{1,3,2,0:T(8,128)S(1)} %get-tuple-element.71, f32[1,64,2,64]{1,3,2,0:T(8,128)S(1)} %get-tuple-element.68), kind=kOutput, calls=%fused_computation.54 | convolution fusion | flops 3223339008 | bytes 21037056 | tf_op jit(solution)/shard_map/abpn,paqk->kbqn/dot_general | solution.py:93
  378.7 22.2 %fusion.8 = f32[64,2,64,256,1]{3,2,0,1,4:T(8,128)} fusion(f32[1,64,64,2,64]{2,4,1,3,0:T(8,128)} %get-tuple-element.64, f32[1,64,64,2,64]{2,4,1,3,0:T(8,128)} %get-tuple-element.65, f32[64,64,2,256,1]{3,0,1,2,4:T(8,128)} %fusion.34), kind=kOutput, calls=%fused_computation.15 | convolution fusion | flops 3222274048 | bytes 20971520 | tf_op jit(solution)/shard_map/kbpn,pkbqm->mkqn/dot_general | solution.py:98
  400.9 4.3 fusion.16
  405.2 4.9 copy.156
  410.0 23.4 %copy.157 = f32[4096,2,256]{2,1,0:T(2,128)} copy(f32[4096,2,256]{2,0,1:T(8,128)S(1)} %bitcast.200) | data formatting | bytes 16777216 | tf_op jit(solution)/shard_map/div | solution.py:144
  433.5 4.7 all-to-all-start
  438.3 8.4 %fusion.55 = (f32[64,64,1,128]{3,1,2,0:T(8,128)S(1)}, f32[64,64,1,128]{3,1,2,0:T(8,128)S(1)}, f32[64,64,1,128]{3,1,2,0:T(8,128)S(1)}) fusion(s32[64]{0:T(128)S(1)} %iota_multiply_fusion.1), kind=kLoop, calls=%fused_computation.80 | loop fusion | flops 8388608 | bytes 6291712 | tf_op jit(solution)/shard_map/sin | solution.py:49
  446.7 4.3 maximum_bitcast_fusion
  451.0 168.5 %all-to-all-done = f32[4096,2,256]{2,1,0:T(2,128)} async-done(((f32[4096,2,256]{2,1,0:T(2,128)}), f32[4096,2,256]{2,1,0:T(2,128)}, u32[]{:S(2)}, u32[]{:S(2)}) %all-to-all-start) | async-done | bytes 8388640 | tf_op jit(solution)/shard_map/all_to_all | solution.py:145
  619.5 7.4 copy.158
  627.0 8.7 %copy.159 = f32[256,2,16,256]{0,3,2,1:T(8,128)} copy(f32[256,2,16,256]{3,0,2,1:T(8,128)} %bitcast.201) | data formatting | bytes 16777216 | tf_op jit(solution)/shard_map/all_to_all | solution.py:145
  635.7 31.7 %convolution_bitcast_fusion = f32[256,2,64,128]{0,3,1,2:T(8,128)} fusion(f32[1,64,64,2,128]{4,2,0,3,1:T(8,128)} %get-tuple-element.61, f32[1,64,64,2,128]{4,2,0,3,1:T(8,128)} %get-tuple-element.60, f32[256,2,64,64,1]{0,3,2,1,4:T(8,128)} %bitcast.195), kind=kOutput, calls=%fused_computation.9 | convolution fusion | flops 6444548096 | bytes 33554432 | tf_op jit(solution)/shard_map/rpmk,pkmqb->rqkb/dot_general | solution.py:111
  667.4 16.9 %copy.161 = f32[256,2,64,128]{3,2,1,0:T(8,128)} copy(f32[256,2,64,128]{0,3,1,2:T(8,128)} %convolution_bitcast_fusion) | data formatting | bytes 33554432 | tf_op jit(solution)/shard_map/rpmk,pkmqb->rqkb/transpose | solution.py:111
  685.0 12.2 %bitcast_multiply_fusion.1 = f32[64,256,128]{2,0,1:T(8,128)S(1)} fusion(f32[256,2,64,128]{3,2,1,0:T(8,128)} %copy.161, f32[1,64,64]{1,2,0:T(8,128)S(1)} %get-tuple-element.87, f32[1,64,64]{1,2,0:T(8,128)S(1)} %get-tuple-element.88), kind=kOutput, calls=%fused_computation.24 | convolution fusion | flops 3223330816 | bytes 25198592 | tf_op jit(solution)/shard_map/rqkb,qka->rab/dot_general | solution.py:114
  697.2 11.9 %fusion.99 = (bf16[256,8192]{1,0:T(8,128)(2,1)S(1)}, f32[256,8192]{1,0:T(8,128)}) fusion(f32[256]{0:T(256)S(1)} %bitcast.214, f32[32,8,64,128]{3,2,1,0:T(8,128)S(1)} %bitcast.197), kind=kLoop, calls=%fused_computation.180 | loop fusion | flops 6291456 | bytes 20972544 | tf_op jit(solution)/shard_map/convert_element_type | solution.py:147
  716.6 8.4 %collective-permute-done.15 = bf16[31,8192]{1,0:T(8,128)(2,1)S(1)} collective-permute-done((bf16[31,8192]{1,0:T(8,128)(2,1)S(1)}, bf16[31,8192]{1,0:T(8,128)(2,1)S(1)}, u32[]{:S(2)}, u32[]{:S(2)}) %collective-permute-start.15) | collective-permute-done | bytes 507936 | tf_op jit(solution)/shard_map/ppermute | solution.py:34
  725.0 3.4 collective-permute-done.16
  728.4 6.4 pad_maximum_fusion.1
  734.8 30.7 %while.10 = (s32[]{:T(128)}, f32[4,64,8,128]{3,2,1,0:T(8,128)}, s32[4]{0:T(128)S(1)}, bf16[318,8192]{1,0:T(8,128)(2,1)}, bf16[512,126]{1,0:T(8,128)(2,1)S(1)}, /*index=5*/s32[]{:T(128)}, s32[]{:T(128)}, s32[]{:T(128)}) while((s32[]{:T(128)}, f32[4,64,8,128]{3,2,1,0:T(8,128)}, s32[4]{0:T(128)S(1)}, bf16[318,8192]{1,0:T(8,128)(2,1)}, ...), condition=%wide.region_3.4_spmd, body=%wide.region_1.3_spmd.sunk | while | flops 1065353216 | bytes 4061831 | solution.py:179
  737.5 4.1 bitcast_reduce_fusion.2
  745.2 4.0 bitcast_reduce_fusion.2
  752.9 4.0 bitcast_reduce_fusion.2
  760.6 4.0 bitcast_reduce_fusion.2
  (110 shorter events, 66.7 us)
Async XLA Ops:
  83.5 44.7 %collective-permute-start = (f32[256,2,256]{2,0,1:T(8,128)}, f32[256,2,256]{2,0,1:T(8,128)}, u32[]{:S(2)}, u32[]{:S(2)}) collective-permute-start(f32[256,2,256]{2,0,1:T(8,128)} %bitcast.209), channel_id=1, source_target_pairs={{0,1},{1,0},{2,3},{3,2},{4,5},{5,4},{6,7},{7,6},{8,9},{9,8},{10,11... | collective-permute-start | bytes 1572872 | tf_op jit(solution)/shard_map/ppermute | solution.py:133
  85.2 47.2 %collective-permute-start.1 = (f32[256,2,256]{2,0,1:T(8,128)}, f32[256,2,256]{2,0,1:T(8,128)}, u32[]{:S(2)}, u32[]{:S(2)}) collective-permute-start(f32[256,2,256]{2,0,1:T(8,128)} %bitcast.32), channel_id=1, source_target_pairs={{0,2},{1,3},{2,0},{3,1},{4,6},{5,7},{6,4},{7,5},{8,10},{9,11},{10,... | collective-permute-start | bytes 1572872 | tf_op jit(solution)/shard_map/ppermute | solution.py:133
  87.4 47.1 %collective-permute-start.2 = (f32[256,2,256]{2,0,1:T(8,128)}, f32[256,2,256]{2,0,1:T(8,128)}, u32[]{:S(2)}, u32[]{:S(2)}) collective-permute-start(f32[256,2,256]{2,0,1:T(8,128)} %bitcast.34), channel_id=1, source_target_pairs={{0,3},{1,2},{2,1},{3,0},{4,7},{5,6},{6,5},{7,4},{8,11},{9,10},{10,... | collective-permute-start | bytes 1572872 | tf_op jit(solution)/shard_map/ppermute | solution.py:133
  88.8 47.6 %collective-permute-start.3 = (f32[256,2,256]{2,0,1:T(8,128)}, f32[256,2,256]{2,0,1:T(8,128)}, u32[]{:S(2)}, u32[]{:S(2)}) collective-permute-start(f32[256,2,256]{2,0,1:T(8,128)} %bitcast.36), channel_id=1, source_target_pairs={{0,4},{1,5},{2,6},{3,7},{4,0},{5,1},{6,2},{7,3},{8,12},{9,13},{10,... | collective-permute-start | bytes 1572872 | tf_op jit(solution)/shard_map/ppermute | solution.py:133
  91.1 12.9 %copy-start.9 = (s32[4096]{0:T(1024)S(1)}, s32[4096]{0:T(1024)}, u32[]{:S(2)}) copy-start(s32[4096]{0:T(1024)} %param.7) | copy-start | bytes 49156
  91.1 49.9 %collective-permute-start.4 = (f32[256,2,256]{2,0,1:T(8,128)}, f32[256,2,256]{2,0,1:T(8,128)}, u32[]{:S(2)}, u32[]{:S(2)}) collective-permute-start(f32[256,2,256]{2,0,1:T(8,128)} %bitcast.38), channel_id=1, source_target_pairs={{0,5},{1,4},{2,7},{3,6},{4,1},{5,0},{6,3},{7,2},{8,13},{9,12},{10,... | collective-permute-start | bytes 1572872 | tf_op jit(solution)/shard_map/ppermute | solution.py:133
  104.0 2.6 copy-start.2
  104.0 3.7 copy-start.3
  107.8 18.4 %copy-start.8 = (f32[256,2,1,256]{0,3,2,1:T(8,128)S(1)}, f32[256,2,1,256]{0,3,2,1:T(8,128)}, u32[]{:S(2)}) copy-start(f32[256,2,1,256]{0,3,2,1:T(8,128)} %get-tuple-element.47) | copy-start | bytes 1572868
  117.4 9.8 %copy-start.7 = (f32[256,2,1,256]{0,3,2,1:T(8,128)S(1)}, f32[256,2,1,256]{0,3,2,1:T(8,128)}, u32[]{:S(2)}) copy-start(f32[256,2,1,256]{0,3,2,1:T(8,128)} %get-tuple-element.46) | copy-start | bytes 1572868
  117.4 10.0 %copy-start.6 = (f32[256,2,1,256]{0,3,2,1:T(8,128)S(1)}, f32[256,2,1,256]{0,3,2,1:T(8,128)}, u32[]{:S(2)}) copy-start(f32[256,2,1,256]{0,3,2,1:T(8,128)} %get-tuple-element.45) | copy-start | bytes 1572868
  117.4 10.2 %copy-start.5 = (f32[256,2,1,256]{0,3,2,1:T(8,128)S(1)}, f32[256,2,1,256]{0,3,2,1:T(8,128)}, u32[]{:S(2)}) copy-start(f32[256,2,1,256]{0,3,2,1:T(8,128)} %get-tuple-element.44) | copy-start | bytes 1572868
  117.4 10.4 %copy-start.4 = (f32[256,2,1,256]{0,3,2,1:T(8,128)S(1)}, f32[256,2,1,256]{0,3,2,1:T(8,128)}, u32[]{:S(2)}) copy-start(f32[256,2,1,256]{0,3,2,1:T(8,128)} %get-tuple-element.43) | copy-start | bytes 1572868
  128.2 30.1 %collective-permute-start.5 = (f32[256,2,256]{2,0,1:T(8,128)}, f32[256,2,256]{2,0,1:T(8,128)S(1)}, u32[]{:S(2)}, u32[]{:S(2)}) collective-permute-start(f32[256,2,256]{2,0,1:T(8,128)} %bitcast.213), channel_id=1, source_target_pairs={{0,6},{1,7},{2,4},{3,5},{4,2},{5,3},{6,0},{7,1},{8,14},{9,15},{10,... | collective-permute-start | bytes 1572872 | tf_op jit(solution)/shard_map/ppermute | solution.py:133
  132.4 37.1 %collective-permute-start.6 = (f32[256,2,256]{2,0,1:T(8,128)}, f32[256,2,256]{2,0,1:T(8,128)S(1)}, u32[]{:S(2)}, u32[]{:S(2)}) collective-permute-start(f32[256,2,256]{2,0,1:T(8,128)} %bitcast.212), channel_id=1, source_target_pairs={{0,7},{1,6},{2,5},{3,4},{4,3},{5,2},{6,1},{7,0},{8,15},{9,14},{10,... | collective-permute-start | bytes 1572872 | tf_op jit(solution)/shard_map/ppermute | solution.py:133
  134.5 37.1 %collective-permute-start.7 = (f32[256,2,256]{2,0,1:T(8,128)}, f32[256,2,256]{2,0,1:T(8,128)S(1)}, u32[]{:S(2)}, u32[]{:S(2)}) collective-permute-start(f32[256,2,256]{2,0,1:T(8,128)} %bitcast.211), channel_id=1, source_target_pairs={{0,8},{1,9},{2,10},{3,11},{4,12},{5,13},{6,14},{7,15},{8,0},{9,1},... | collective-permute-start | bytes 1572872 | tf_op jit(solution)/shard_map/ppermute | solution.py:133
  136.4 88.3 %collective-permute-start.8 = (f32[256,2,256]{2,0,1:T(8,128)}, f32[256,2,256]{2,0,1:T(8,128)S(1)}, u32[]{:S(2)}, u32[]{:S(2)}) collective-permute-start(f32[256,2,256]{2,0,1:T(8,128)} %bitcast.210), channel_id=1, source_target_pairs={{0,9},{1,8},{2,11},{3,10},{4,13},{5,12},{6,15},{7,14},{8,1},{9,0},... | collective-permute-start | bytes 1572872 | tf_op jit(solution)/shard_map/ppermute | solution.py:133
  141.0 106.2 %collective-permute-start.9 = (f32[256,2,256]{2,0,1:T(8,128)}, f32[256,2,256]{2,0,1:T(8,128)S(1)}, u32[]{:S(2)}, u32[]{:S(2)}) collective-permute-start(f32[256,2,256]{2,0,1:T(8,128)} %bitcast.208), channel_id=1, source_target_pairs={{0,10},{1,11},{2,8},{3,9},{4,14},{5,15},{6,12},{7,13},{8,2},{9,3},... | collective-permute-start | bytes 1572872 | tf_op jit(solution)/shard_map/ppermute | solution.py:133
  158.3 111.3 %collective-permute-start.10 = (f32[256,2,256]{2,0,1:T(8,128)S(1)}, f32[256,2,256]{2,0,1:T(8,128)S(1)}, u32[]{:S(2)}, u32[]{:S(2)}) collective-permute-start(f32[256,2,256]{2,0,1:T(8,128)S(1)} %bitcast.207), channel_id=1, source_target_pairs={{0,11},{1,10},{2,9},{3,8},{4,15},{5,14},{6,13},{7,12},{8,3},{9,2},... | collective-permute-start | bytes 1572872 | tf_op jit(solution)/shard_map/ppermute | solution.py:133
  169.5 114.4 %collective-permute-start.11 = (f32[256,2,256]{2,0,1:T(8,128)S(1)}, f32[256,2,256]{2,0,1:T(8,128)S(1)}, u32[]{:S(2)}, u32[]{:S(2)}) collective-permute-start(f32[256,2,256]{2,0,1:T(8,128)S(1)} %bitcast.206), channel_id=1, source_target_pairs={{0,12},{1,13},{2,14},{3,15},{4,8},{5,9},{6,10},{7,11},{8,4},{9,5},... | collective-permute-start | bytes 1572872 | tf_op jit(solution)/shard_map/ppermute | solution.py:133
  171.7 124.5 %collective-permute-start.12 = (f32[256,2,256]{2,0,1:T(8,128)S(1)}, f32[256,2,256]{2,0,1:T(8,128)S(1)}, u32[]{:S(2)}, u32[]{:S(2)}) collective-permute-start(f32[256,2,256]{2,0,1:T(8,128)S(1)} %bitcast.205), channel_id=1, source_target_pairs={{0,13},{1,12},{2,15},{3,14},{4,9},{5,8},{6,11},{7,10},{8,5},{9,4},... | collective-permute-start | bytes 1572872 | tf_op jit(solution)/shard_map/ppermute | solution.py:133
  224.7 82.6 %collective-permute-start.13 = (f32[256,2,256]{2,0,1:T(8,128)S(1)}, f32[256,2,256]{2,0,1:T(8,128)S(1)}, u32[]{:S(2)}, u32[]{:S(2)}) collective-permute-start(f32[256,2,256]{2,0,1:T(8,128)S(1)} %bitcast.204), channel_id=1, source_target_pairs={{0,14},{1,15},{2,12},{3,13},{4,10},{5,11},{6,8},{7,9},{8,6},{9,7},... | collective-permute-start | bytes 1572872 | tf_op jit(solution)/shard_map/ppermute | solution.py:133
  247.2 71.7 %collective-permute-start.14 = (f32[256,2,256]{2,0,1:T(8,128)S(1)}, f32[256,2,256]{2,0,1:T(8,128)S(1)}, u32[]{:S(2)}, u32[]{:S(2)}) collective-permute-start(f32[256,2,256]{2,0,1:T(8,128)S(1)} %bitcast.203), channel_id=1, source_target_pairs={{0,15},{1,14},{2,13},{3,12},{4,11},{5,10},{6,9},{7,8},{8,7},{9,6},... | collective-permute-start | bytes 1572872 | tf_op jit(solution)/shard_map/ppermute | solution.py:133
  344.7 22.1 %copy-start.1 = (f32[64,64,256]{2,0,1:T(8,128)S(1)}, f32[64,64,256]{2,0,1:T(8,128)}, u32[]{:S(2)}) copy-start(f32[64,64,256]{2,0,1:T(8,128)} %compare_convert_fusion) | copy-start | bytes 12582916
  433.5 186.0 %all-to-all-start = ((f32[4096,2,256]{2,1,0:T(2,128)}), f32[4096,2,256]{2,1,0:T(2,128)}, u32[]{:S(2)}, u32[]{:S(2)}) async-start(f32[4096,2,256]{2,1,0:T(2,128)} %copy.157), calls=%async_computation | async-start | bytes 16777216 | tf_op jit(solution)/shard_map/all_to_all | solution.py:145
  697.2 18.8 %copy-start.10 = (f32[8,32]{1,0:T(8,128)S(1)}, f32[8,32]{1,0:T(8,128)}, u32[]{:S(2)}) copy-start(f32[8,32]{1,0:T(8,128)} %param.9) | copy-start | bytes 3076
  697.2 18.8 %copy-start.11 = (s32[8,32]{1,0:T(8,128)S(1)}, s32[8,32]{1,0:T(8,128)}, u32[]{:S(2)}) copy-start(s32[8,32]{1,0:T(8,128)} %param.8) | copy-start | bytes 3076
  709.1 2.0 copy-start
  711.2 13.8 %collective-permute-start.15 = (bf16[31,8192]{1,0:T(8,128)(2,1)S(1)}, bf16[31,8192]{1,0:T(8,128)(2,1)S(1)}, u32[]{:S(2)}, u32[]{:S(2)}) collective-permute-start(bf16[31,8192]{1,0:T(8,128)(2,1)S(1)} %get-tuple-element.58), channel_id=1, source_target_pairs={{0,1},{1,2},{2,3},{3,4},{4,5},{5,6},{6,7},{7,8},{8,9},{9,10},{10,1... | collective-permute-start | bytes 1523720 | tf_op jit(solution)/shard_map/ppermute | solution.py:34
  713.3 15.2 %collective-permute-start.16 = (bf16[31,8192]{1,0:T(8,128)(2,1)S(1)}, bf16[31,8192]{1,0:T(8,128)(2,1)S(1)}, u32[]{:S(2)}, u32[]{:S(2)}) collective-permute-start(bf16[31,8192]{1,0:T(8,128)(2,1)S(1)} %get-tuple-element.59), channel_id=1, source_target_pairs={{1,0},{2,1},{3,2},{4,3},{5,4},{6,5},{7,6},{8,7},{9,8},{10,9},{11,1... | collective-permute-start | bytes 1523720 | tf_op jit(solution)/shard_map/ppermute | solution.py:35
